TPU v7x, 32 devices: a whole 2x2x4 slice. The times are simulated.
32 devices in a mesh: groups: 2 (over y), replica: 4 (over z), tensor: 4 (over x, core).
Axes of the slice: x: 2, y: 2, z: 4, core: 2. Of those that a mesh axis runs over, the one named last changes fastest.
Arguments:
- queries: bfloat16 [144, 8192], P(('groups', 'replica'), 'tensor'), parts along dimension 0, may hold values from -64 to 64
- past_cache: bfloat16 [2, 144, 128, 1024], P(None, ('groups', 'replica'), None, 'tensor'), parts along dimension 1, may hold values from -6 to 6
- lengths: int32 [144], P(('groups', 'replica')), parts along dimension 0, may hold values from 2 to 128, as said below
- live_counts: int32 [8], P(('groups', 'replica')), parts along dimension 0, may hold values from 1 to 16, as said below
- adapter_index: int32 [144], P(('groups', 'replica')), parts along dimension 0, may hold values from 0 to 15, as said below
- adapter_down: bfloat16 [16, 16, 8192], P('replica', None, 'tensor'), may hold values from -0.0625 to 0.0625
- adapter_up: bfloat16 [16, 16, 8192], P('replica', None, 'tensor'), may hold values from -6 to 6
Outputs:
- attention: bfloat16 [144, 8192], P(('groups', 'replica'), 'tensor'), parts along dimension 0
- adapted: bfloat16 [144, 8192], P(('groups', 'replica'), 'tensor'), parts along dimension 0
There are 2 independent parts, one for each index of `groups`. A program takes and returns all parts, laid end to end along the dimension named above; an argument that names none is the same for every part. Nothing has to cross between parts.
Inputs may be any that keep to these rules, and one draw needn't show every extreme that they name: `adapter_index`: over the first 16 slots of all replicas, exactly 4 distinct adapters appear, homed on 4 distinct replicas. Each of the last 2 slots of a replica names an adapter outside that set; the homes (adapter a lives on replica a // 4) of one replica's last 2 slots are distinct, and some replica is the home of one such slot of every replica. `lengths`: some request has exactly 128. `live_counts`: some replica has exactly 16.
All inputs are finite; a program needn't handle non-finite values.
Results may differ from a plain program's by a relative error of at most 0.008.
Values may be sent and summed in bfloat16 or wider, within the bound.
A program may use at most 64 MiB of HBM per device.

v0:
```python
import functools
import math

import jax
import jax.numpy as jnp
from jax import lax
from jax.experimental import pallas as pl
from jax.experimental.pallas import tpu as pltpu
from jax.sharding import PartitionSpec as P

HEAD_DIM = 128
STAY = 16
SCALING = 2.0
GROUP = 4
REACH = 2
LIMIT = 67043328 - 240 * 1024
MESH = pl.DeviceIdType.MESH
F32 = jnp.float32
BF16 = jnp.bfloat16


def dot_nt(a, b):
    return lax.dot_general(a, b, (((1,), (1,)), ((), ())), preferred_element_type=F32)


def dot_nn(a, b):
    return lax.dot_general(a, b, (((1,), (0,)), ((), ())), preferred_element_type=F32)


def widen(ranks, up):
    high = ranks.astype(BF16)
    low = (ranks - high.astype(F32)).astype(BF16)
    return SCALING * (dot_nn(high, up) + dot_nn(low, up))


def kernel(
    replicas, tensors,
    lengths, live, index, queries, cache, down, up,
    attention, adapted,
    q_in, kv, down_v, up_v, q_rows, o_rows,
    idx_buf, row_out, row_in, row_send, row_back, hot_down, hot_up, rank_m, rank_s,
    local_sem, group_sem,
    idx_s, idx_r, row_s, row_r, back_s, back_r, hd_s, hd_r, hu_s, hu_r, tm_s, tm_r, ts_s, ts_r,
):
    me = lax.axis_index("replica")
    mine = lax.axis_index("tensor")
    slots, cols = queries.shape
    moving = slots - STAY
    context = cache.shape[2]
    key_heads = cache.shape[3] // HEAD_DIM
    heads = cols // HEAD_DIM
    size = heads // key_heads
    count, rank = down.shape[0], down.shape[1]
    groups = STAY // GROUP

    def peer(offset):
        return {"replica": lax.rem(me + offset, replicas)}

    def side(offset):
        return {"tensor": lax.rem(mine + offset, tensors)}

    barrier = pltpu.get_barrier_semaphore()
    for d in range(1, replicas):
        pl.semaphore_signal(barrier, inc=1, device_id=peer(d), device_id_type=MESH)
    for d in range(1, tensors):
        pl.semaphore_signal(barrier, inc=1, device_id=side(d), device_id_type=MESH)

    load_q = pltpu.make_async_copy(queries, q_in, local_sem.at[0])
    load_m = pltpu.make_async_copy(
        cache.at[:, pl.ds(STAY, moving)], kv.at[:, pl.ds(STAY, moving)], local_sem.at[1]
    )
    load_d = pltpu.make_async_copy(down, down_v, local_sem.at[2])
    load_u = pltpu.make_async_copy(up, up_v, local_sem.at[3])
    loads = [
        pltpu.make_async_copy(
            cache.at[:, pl.ds(g * GROUP, GROUP)], kv.at[:, pl.ds(g * GROUP, GROUP)], group_sem.at[g]
        )
        for g in range(groups)
    ]
    load_q.start()
    load_m.start()
    for copy in loads[:2]:
        copy.start()
    load_d.start()
    load_u.start()
    for copy in loads[2:]:
        copy.start()

    def to_peers(source, target, send, recv):
        return [
            pltpu.make_async_remote_copy(
                src_ref=source(d), dst_ref=target.at[d], send_sem=send.at[d - 1],
                recv_sem=recv.at[d - 1], device_id=peer(d), device_id_type=MESH,
            )
            for d in range(1, replicas)
        ]

    def to_sides(buffer, send, recv):
        return [
            pltpu.make_async_remote_copy(
                src_ref=buffer.at[0], dst_ref=buffer.at[d], send_sem=send.at[d - 1],
                recv_sem=recv.at[d - 1], device_id=side(d), device_id_type=MESH,
            )
            for d in range(1, tensors)
        ]

    send_idx = to_peers(lambda d: idx_buf.at[0], idx_buf, idx_s, idx_r)
    send_rows = to_peers(lambda d: row_out.at[d], row_in, row_s, row_r)
    send_hd = to_peers(lambda d: hot_down.at[0], hot_down, hd_s, hd_r)
    send_hu = to_peers(lambda d: hot_up.at[0], hot_up, hu_s, hu_r)

    def straight(d):
        return ((me + d < replicas) & (d <= REACH)) | ((me + d >= replicas) & (replicas - d <= REACH))

    def onward(buffer, send, recv):
        steps = {}
        for d in range(1, replicas):
            options = []
            if d >= REACH and d + 1 < replicas:
                options.append(((me >= d) & (me + 1 < replicas), 1, d + 1, replicas - 1))
            if replicas - d >= REACH and d > 1:
                options.append(((me < d) & (me >= 1), replicas - 1, d - 1, 2 * (replicas - 1)))
            steps[d] = [
                (flag, pltpu.make_async_remote_copy(
                    src_ref=buffer.at[d], dst_ref=buffer.at[slot], send_sem=send.at[base + d - 1],
                    recv_sem=recv.at[slot - 1], device_id=peer(step), device_id_type=MESH,
                ))
                for flag, step, slot, base in options
            ]
        return steps

    pass_hd = onward(hot_down, hd_s, hd_r)
    pass_hu = onward(hot_up, hu_s, hu_r)
    order = sorted(range(1, replicas), key=lambda d: (not pass_hd[d], d))

    def start_if(flag, copy):
        @pl.when(flag)
        def _():
            copy.start()

    def sent_if(flag, copy):
        @pl.when(flag)
        def _():
            copy.wait_send()

    def spread(sends):
        for d in order:
            start_if(straight(d), sends[d - 1])

    def relay(sends, passes):
        for d in order:
            if passes[d]:
                sends[d - 1].wait_recv()
                for flag, copy in passes[d]:
                    start_if(flag, copy)

    def settle(sends, passes):
        for d in order:
            if not passes[d]:
                sends[d - 1].wait_recv()
    send_back = [
        pltpu.make_async_remote_copy(
            src_ref=row_send.at[d], dst_ref=row_back.at[d], send_sem=back_s.at[d - 1],
            recv_sem=back_r.at[d - 1], device_id=peer(replicas - d), device_id_type=MESH,
        )
        for d in range(1, replicas)
    ]
    send_tm = to_sides(rank_m, tm_s, tm_r)
    send_ts = to_sides(rank_s, ts_s, ts_r)

    lane = lax.broadcasted_iota(jnp.int32, (1, 128), 1)
    line = jnp.full((1, 128), -1, jnp.int32)
    for i in range(slots):
        line = jnp.where(lane == i, index[i], line)
    idx_buf[0] = line
    stay_row = lax.broadcasted_iota(jnp.int32, (STAY, 1), 0)
    stay_rel = jnp.zeros((STAY, 1), jnp.int32)
    for i in range(STAY):
        stay_rel = jnp.where(stay_row == i, lax.rem(me - index[i] // count + replicas, replicas), stay_rel)
    move_rel = [lax.rem(index[STAY + j] // count - me + replicas, replicas) for j in range(moving)]

    load_q.wait()
    for h in range(heads):
        q_rows[pl.ds(h, slots, stride=heads), :] = q_in[:, h * HEAD_DIM:(h + 1) * HEAD_DIM].astype(F32)

    head_row = lax.broadcasted_iota(jnp.int32, (heads, 1), 0) // size
    position = lax.broadcasted_iota(jnp.int32, (1, context), 1)

    def attend(requests):
        for n in requests:
            q = q_rows[n * heads:(n + 1) * heads, :]
            wide = jnp.concatenate(
                [jnp.where(head_row == g, q, 0.0) for g in range(key_heads)], axis=1
            ).astype(BF16)
            scores = dot_nt(wide, kv[0, n]) / math.sqrt(HEAD_DIM)
            scores = jnp.where(position < lengths[n], scores, -jnp.inf)
            peak = jnp.max(scores, axis=-1, keepdims=True)
            raised = jnp.exp(scores - peak)
            weights = (raised / jnp.sum(raised, axis=-1, keepdims=True)).astype(BF16)
            mixed = dot_nn(weights, kv[1, n])
            out = jnp.zeros((heads, HEAD_DIM), F32)
            for g in range(key_heads):
                out = jnp.where(head_row == g, mixed[:, g * HEAD_DIM:(g + 1) * HEAD_DIM], out)
            o_rows[n * heads:(n + 1) * heads, :] = out

    def gather_rows(first, number):
        return jnp.concatenate(
            [o_rows[pl.ds(first * heads + h, number, stride=heads), :] for h in range(heads)], axis=1
        )

    load_m.wait()
    attend(range(STAY, slots))
    moved = gather_rows(STAY, moving).astype(BF16)
    attention[STAY:slots, :] = moved
    moved = moved.astype(F32)
    replica_row = lax.broadcasted_iota(jnp.int32, (replicas, 1), 0)
    picked = jnp.zeros((replicas, cols), F32)
    for j in range(moving):
        picked = jnp.where(replica_row == move_rel[j], moved[j:j + 1, :], picked)
    row_in[0] = picked[0:1, :]
    for d in range(1, replicas):
        row_out[d] = picked[d:d + 1, :]

    pl.semaphore_wait(barrier, replicas - 1 + tensors - 1)
    for copy in send_idx:
        copy.start()
    for copy in send_rows:
        copy.start()

    for g in range(groups // 2):
        loads[g].wait()
        attend(range(g * GROUP, (g + 1) * GROUP))

    load_d.wait()
    load_u.wait()
    for copy in send_idx:
        copy.wait_recv()
    table = jnp.concatenate([idx_buf[d] for d in range(replicas)], axis=0)
    here = (table >= 0) & (table // count == me)
    local = jnp.where(here, table - me * count, -1)
    lanes = lax.broadcasted_iota(jnp.int32, table.shape, 1)
    hot = jnp.maximum(jnp.max(jnp.where(lanes < STAY, local, -1)), 0)
    hot_down[0] = down_v[hot]
    hot_up[0] = up_v[hot]
    spread(send_hd)

    asked = jnp.max(jnp.where(lanes >= STAY, local, -1), axis=1, keepdims=True)
    for copy in send_rows:
        copy.wait_recv()
    rows = jnp.concatenate([row_in[d] for d in range(replicas)], axis=0).astype(BF16)
    partial = dot_nt(rows, down_v[...].reshape(count * rank, cols))
    owner = lax.broadcasted_iota(jnp.int32, partial.shape, 1) // rank
    rank_m[0] = jnp.where(owner == asked, partial, 0.0)
    for copy in send_tm:
        copy.start()

    middle = (groups // 2 + groups) // 2
    for g in range(groups // 2, middle):
        loads[g].wait()
        attend(range(g * GROUP, (g + 1) * GROUP))

    relay(send_hd, pass_hd)
    spread(send_hu)

    for copy in send_tm:
        copy.wait_recv()
    total = rank_m[0]
    for d in range(1, tensors):
        total = total + rank_m[d]
    made = widen(total, up_v[...].reshape(count * rank, cols)).astype(BF16).astype(F32)
    row_back[0] = made[0:1, :]
    for d in range(1, replicas):
        row_send[d] = made[d:d + 1, :]
    for copy in send_back:
        copy.start()

    for g in range(middle, groups):
        loads[g].wait()
        attend(range(g * GROUP, (g + 1) * GROUP))
    stay = jnp.where(stay_row < live[0], gather_rows(0, STAY), 0.0).astype(BF16)
    attention[0:STAY, :] = stay

    settle(send_hd, pass_hd)
    partial = dot_nt(stay, hot_down[...].reshape(replicas * rank, cols))
    owner = lax.broadcasted_iota(jnp.int32, partial.shape, 1) // rank
    rank_s[0] = jnp.where(owner == stay_rel, partial, 0.0)
    for copy in send_ts:
        copy.start()

    relay(send_hu, pass_hu)
    for copy in send_back:
        copy.wait_recv()
    back = jnp.concatenate([row_back[d] for d in range(replicas)], axis=0)
    adapted[STAY:slots, :] = jnp.concatenate(
        [
            jnp.sum(jnp.where(replica_row == move_rel[j], back, 0.0), axis=0, keepdims=True)
            for j in range(moving)
        ],
        axis=0,
    ).astype(BF16)

    for copy in send_ts:
        copy.wait_recv()
    total = rank_s[0]
    for d in range(1, tensors):
        total = total + rank_s[d]
    settle(send_hu, pass_hu)
    adapted[0:STAY, :] = widen(total, hot_up[...].reshape(replicas * rank, cols)).astype(BF16)

    for copy in send_idx + send_rows + send_back + send_tm + send_ts:
        copy.wait_send()
    for d in order:
        for copies, passes in ((send_hd, pass_hd), (send_hu, pass_hu)):
            sent_if(straight(d), copies[d - 1])
            for flag, copy in passes[d]:
                sent_if(flag, copy)


def hand_over(attention, adapted, attention_out, adapted_out, sem):
    first = pltpu.make_async_copy(attention, attention_out, sem.at[0])
    second = pltpu.make_async_copy(adapted, adapted_out, sem.at[1])
    first.start()
    second.start()
    first.wait()
    second.wait()


def on_device(replicas, tensors, queries, past_cache, lengths, live_counts, adapter_index, adapter_down, adapter_up):
    slots, cols = queries.shape
    count, rank = adapter_down.shape[0], adapter_down.shape[1]
    heads = cols // HEAD_DIM
    out = jax.ShapeDtypeStruct((slots, cols), BF16)
    held = pltpu.VMEM((slots, cols), BF16)
    smem = pl.BlockSpec(memory_space=pltpu.SMEM)
    anywhere = pl.BlockSpec(memory_space=pl.ANY)
    vmem = pl.BlockSpec(memory_space=pltpu.VMEM)
    dma = pltpu.SemaphoreType.DMA
    rep = dma((max(replicas - 1, 1),))
    ten = dma((max(tensors - 1, 1),))
    three = dma((max(3 * (replicas - 1), 1),))
    scratch = [
        pltpu.VMEM((slots, cols), BF16),
        pltpu.VMEM(past_cache.shape, BF16),
        pltpu.VMEM(adapter_down.shape, BF16),
        pltpu.VMEM(adapter_up.shape, BF16),
        pltpu.VMEM((slots * heads, HEAD_DIM), F32),
        pltpu.VMEM((slots * heads, HEAD_DIM), F32),
        pltpu.VMEM((replicas, 1, 128), jnp.int32),
        pltpu.VMEM((replicas, 1, cols), F32),
        pltpu.VMEM((replicas, 1, cols), F32),
        pltpu.VMEM((replicas, 1, cols), F32),
        pltpu.VMEM((replicas, 1, cols), F32),
        pltpu.VMEM((replicas, rank, cols), BF16),
        pltpu.VMEM((replicas, rank, cols), BF16),
        pltpu.VMEM((tensors, replicas, count * rank), F32),
        pltpu.VMEM((tensors, STAY, replicas * rank), F32),
        dma((4,)),
        dma((STAY // GROUP,)),
        rep, rep, rep, rep, rep, rep, three, rep, three, rep, ten, ten, ten, ten,
    ]
    results = pl.pallas_call(
        functools.partial(kernel, replicas, tensors),
        out_shape=(held, held),
        in_specs=[smem, smem, smem, anywhere, anywhere, anywhere, anywhere],
        out_specs=(vmem, vmem),
        scratch_shapes=scratch,
        compiler_params=pltpu.CompilerParams(collective_id=0, has_side_effects=True, vmem_limit_bytes=LIMIT),
    )(lengths, live_counts, adapter_index, queries, past_cache, adapter_down, adapter_up)
    return pl.pallas_call(
        hand_over,
        out_shape=(out, out),
        in_specs=[vmem, vmem],
        out_specs=(anywhere, anywhere),
        scratch_shapes=[dma((2,))],
        compiler_params=pltpu.CompilerParams(vmem_limit_bytes=4 * 1024 * 1024),
    )(*results)


def solution(mesh):
    in_specs = (
        P(("groups", "replica"), "tensor"),
        P(None, ("groups", "replica"), None, "tensor"),
        P(("groups", "replica")),
        P(("groups", "replica")),
        P(("groups", "replica")),
        P("replica", None, "tensor"),
        P("replica", None, "tensor"),
    )
    out_specs = (P(("groups", "replica"), "tensor"), P(("groups", "replica"), "tensor"))
    body = functools.partial(on_device, mesh.shape["replica"], mesh.shape["tensor"])
    return jax.shard_map(body, mesh=mesh, in_specs=in_specs, out_specs=out_specs, check_vma=False)
```

profile of v0, /device:TPU:0, one launch (start us, length us, event | category | flops | bytes accessed | tf_op | source)
XLA Modules:
  0.0 23.8 jit_solution(11976554263627814914)
XLA Ops:
  1.3 21.9 %shard_map.86 = (bf16[18,2048]{1,0:T(8,128)(2,1)S(1)}, bf16[18,2048]{1,0:T(8,128)(2,1)S(1)}) custom-call(s32[18]{0:T(128)} %lengths.1, s32[1]{0:T(128)S(6)} %copy.9.live, s32[18]{0:T(128)} %index.1, bf16[18,2048]{1,0:T(8,128)(2,1)} %queries.1, bf16[2,18,128,256]{3,2,1,0:T(8,128)(2,1)} %cache.1, bf16[4,16,2048]{2,1,0:T(8,128)(2,1)} %down.1, ...), custom_call_target="tpu_custom_call" | custom-call | tf_op jit(solution)/shard_map/pallas_call | solution.py:361
  23.1 0.7 %shard_map.87 = (bf16[18,2048]{1,0:T(8,128)(2,1)}, bf16[18,2048]{1,0:T(8,128)(2,1)}) custom-call(bf16[18,2048]{1,0:T(8,128)(2,1)S(1)} %get-tuple-element.4.attention, bf16[18,2048]{1,0:T(8,128)(2,1)S(1)} %get-tuple-element.5.adapted), custom_call_target="tpu_custom_call" | custom-call | tf_op jit(solution)/shard_map/pallas_call | solution.py:369
where the time goes:
time: 24 us; the launch traced here: 23.8 us
  Pallas kernels  22.5 us (94%)
  between operations  1.29 us (5%)
    pallas_call x1, Pallas kernels, on_device(): pl.pallas_call(functools.partial(kernel, replicas, tensors), out_shape=(h...  21.9 us
    pallas_call x1, Pallas kernels, on_device(): pl.pallas_call(hand_over, out_shape=(out, out), in_specs=[vmem, vmem], ou...  0.69 us

commit v1 on v0

v1 whole, which is shorter than its diff:
```python
import functools
import math

import jax
import jax.numpy as jnp
from jax import lax
from jax.experimental import pallas as pl
from jax.experimental.pallas import tpu as pltpu
from jax.sharding import PartitionSpec as P

HEAD_DIM = 128
STAY = 16
SCALING = 2.0
GROUP = 8
EARLY = 1
LIMIT = 67043328 - 240 * 1024
MESH = pl.DeviceIdType.MESH
F32 = jnp.float32
BF16 = jnp.bfloat16


def dot_nt(a, b):
    return lax.dot_general(a, b, (((1,), (1,)), ((), ())), preferred_element_type=F32)


def dot_nn(a, b):
    return lax.dot_general(a, b, (((1,), (0,)), ((), ())), preferred_element_type=F32)


def widen(ranks, up):
    high = ranks.astype(BF16)
    low = (ranks - high.astype(F32)).astype(BF16)
    return SCALING * (dot_nn(high, up) + dot_nn(low, up))


def kernel(
    replicas, tensors,
    lengths_in, live_in, index_in, queries, cache, down, up,
    attention, adapted,
    lengths, live, index, hot, q_in, kv, down_v, up_v, q_rows, o_rows,
    row_out, row_in, row_send, row_back, out_down, hot_down, hot_up, stay_out, stay_in, rank_m, rank_s, rank_e,
    local_sem, group_sem,
    idx_s, idx_r, row_s, row_r, back_s, back_r, hd_s, hd_r, hu_s, hu_r, tm_s, tm_r, ts_s, ts_r, te_s, st_s, st_r,
):
    me = lax.axis_index("replica")
    mine = lax.axis_index("tensor")
    slots, cols = queries.shape
    moving = slots - STAY
    context = cache.shape[2]
    key_heads = cache.shape[3] // HEAD_DIM
    heads = cols // HEAD_DIM
    size = heads // key_heads
    count, rank = down.shape[0], down.shape[1]
    groups = STAY // GROUP
    last = replicas - 1
    edge = (me == 0) | (me == last)
    inner = jnp.logical_not(edge)
    proxy = (me == 1) | (me == last - 1)
    helper = jnp.where(me == 0, 1, last - 1)
    served = jnp.where(me == 1, 0, last)

    def peer(offset):
        return {"replica": lax.rem(me + offset, replicas)}

    def side(offset):
        return {"tensor": lax.rem(mine + offset, tensors)}

    barrier = pltpu.get_barrier_semaphore()
    for d in range(1, replicas):
        pl.semaphore_signal(barrier, inc=1, device_id=peer(d), device_id_type=MESH)
    for d in range(1, tensors):
        pl.semaphore_signal(barrier, inc=1, device_id=side(d), device_id_type=MESH)

    @pl.when(edge)
    def _():
        for d in range(1, tensors):
            pl.semaphore_signal(
                barrier, inc=1, device_id={"replica": helper, **side(d)}, device_id_type=MESH
            )

    load_i = pltpu.make_async_copy(index_in, index.at[0], local_sem.at[0])
    load_n = pltpu.make_async_copy(lengths_in, lengths, local_sem.at[1])
    load_l = pltpu.make_async_copy(live_in, live, local_sem.at[2])
    load_q = pltpu.make_async_copy(queries, q_in, local_sem.at[3])
    load_m = pltpu.make_async_copy(
        cache.at[:, pl.ds(STAY, moving)], kv.at[:, pl.ds(STAY, moving)], local_sem.at[4]
    )
    load_d = pltpu.make_async_copy(down, down_v, local_sem.at[5])
    load_u = pltpu.make_async_copy(up, up_v, local_sem.at[6])
    loads = [
        pltpu.make_async_copy(
            cache.at[:, pl.ds(g * GROUP, GROUP)], kv.at[:, pl.ds(g * GROUP, GROUP)], group_sem.at[g]
        )
        for g in range(groups)
    ]
    load_q.start()
    load_m.start()
    load_i.start()
    load_n.start()
    load_l.start()
    for copy in loads[:2]:
        copy.start()
    load_d.start()
    load_u.start()
    for copy in loads[2:]:
        copy.start()

    def to_peers(source, target, send, recv):
        return [
            pltpu.make_async_remote_copy(
                src_ref=source(d), dst_ref=target.at[d], send_sem=send.at[d - 1],
                recv_sem=recv.at[d - 1], device_id=peer(d), device_id_type=MESH,
            )
            for d in range(1, replicas)
        ]

    def to_sides(buffer, send, recv):
        return [
            pltpu.make_async_remote_copy(
                src_ref=buffer.at[0], dst_ref=buffer.at[d], send_sem=send.at[d - 1],
                recv_sem=recv.at[d - 1], device_id=side(d), device_id_type=MESH,
            )
            for d in range(1, tensors)
        ]

    send_idx = to_peers(lambda d: index.at[0], index, idx_s, idx_r)
    send_rows = to_peers(lambda d: row_out.at[d], row_in, row_s, row_r)
    send_back = [
        pltpu.make_async_remote_copy(
            src_ref=row_send.at[d], dst_ref=row_back.at[d], send_sem=back_s.at[d - 1],
            recv_sem=back_r.at[d - 1], device_id=peer(replicas - d), device_id_type=MESH,
        )
        for d in range(1, replicas)
    ]
    send_tm = to_sides(rank_m, tm_s, tm_r)
    send_ts = [
        pltpu.make_async_remote_copy(
            src_ref=rank_s.at[0], dst_ref=rank_s.at[d], send_sem=ts_s.at[d],
            recv_sem=ts_r.at[d], device_id=side(d), device_id_type=MESH,
        )
        for d in range(1, tensors)
    ]
    send_te = [
        pltpu.make_async_remote_copy(
            src_ref=rank_e, dst_ref=rank_s.at[d], send_sem=te_s.at[d],
            recv_sem=ts_r.at[d], device_id={"replica": served, **side(d)}, device_id_type=MESH,
        )
        for d in range(tensors)
    ]
    send_stay = pltpu.make_async_remote_copy(
        src_ref=stay_out, dst_ref=stay_in, send_sem=st_s, recv_sem=st_r,
        device_id={"replica": helper}, device_id_type=MESH,
    )
    send_hu = to_peers(lambda d: hot_up.at[0], hot_up, hu_s, hu_r)

    def down_to(d, k):
        return pltpu.make_async_remote_copy(
            src_ref=out_down.at[k - 1], dst_ref=hot_down.at[d], send_sem=hd_s.at[d - 1],
            recv_sem=hd_r.at[d - 1], device_id=peer(d), device_id_type=MESH,
        )

    def at_end(d):
        target = lax.rem(me + d, replicas)
        return (target == 0) | (target == last)

    def start_if(flag, copy):
        @pl.when(flag)
        def _():
            copy.start()

    def sent_if(flag, copy):
        @pl.when(flag)
        def _():
            copy.wait_send()

    load_q.wait()
    for h in range(heads):
        q_rows[pl.ds(h, slots, stride=heads), :] = q_in[:, h * HEAD_DIM:(h + 1) * HEAD_DIM].astype(F32)

    head_row = lax.broadcasted_iota(jnp.int32, (heads, 1), 0) // size
    position = lax.broadcasted_iota(jnp.int32, (1, context), 1)
    scale = 1.0 / math.sqrt(HEAD_DIM)

    def attend(requests):
        requests = list(requests)
        scores = []
        for n in requests:
            q = q_rows[n * heads:(n + 1) * heads, :]
            wide = jnp.concatenate(
                [jnp.where(head_row == g, q, 0.0) for g in range(key_heads)], axis=1
            ).astype(BF16)
            scores.append(jnp.where(position < lengths[n], dot_nt(wide, kv[0, n]) * scale, -jnp.inf))
        scores = jnp.concatenate(scores, axis=0)
        peak = jnp.max(scores, axis=-1, keepdims=True)
        raised = jnp.exp(scores - peak)
        weights = (raised / jnp.sum(raised, axis=-1, keepdims=True)).astype(BF16)
        for i, n in enumerate(requests):
            mixed = dot_nn(weights[i * heads:(i + 1) * heads, :], kv[1, n])
            out = mixed[:, :HEAD_DIM]
            for g in range(1, key_heads):
                out = jnp.where(head_row == g, mixed[:, g * HEAD_DIM:(g + 1) * HEAD_DIM], out)
            o_rows[n * heads:(n + 1) * heads, :] = out

    def gather_rows(first, number):
        return jnp.concatenate(
            [o_rows[pl.ds(first * heads + h, number, stride=heads), :] for h in range(heads)], axis=1
        )

    load_i.wait()
    load_n.wait()
    load_l.wait()
    stay_row = lax.broadcasted_iota(jnp.int32, (STAY, 1), 0)
    stay_home = jnp.zeros((STAY, 1), jnp.int32)
    for i in range(STAY):
        stay_home = jnp.where(stay_row == i, index[0, i] // count, stay_home)
    move_rel = [lax.rem(index[0, STAY + j] // count - me + replicas, replicas) for j in range(moving)]

    load_m.wait()
    attend(range(STAY, slots))
    moved = gather_rows(STAY, moving).astype(BF16)
    attention[STAY:slots, :] = moved
    moved = moved.astype(F32)
    replica_row = lax.broadcasted_iota(jnp.int32, (replicas, 1), 0)
    picked = jnp.zeros((replicas, cols), F32)
    for j in range(moving):
        picked = jnp.where(replica_row == move_rel[j], moved[j:j + 1, :], picked)
    row_in[0] = picked[0:1, :]
    for d in range(1, replicas):
        row_out[d] = picked[d:d + 1, :]

    def homed(slot, slot_range):
        best = jnp.int32(-1)
        for i in slot_range:
            local = index[slot, i] - me * count
            best = jnp.maximum(best, jnp.where((local >= 0) & (local < count), local, -1))
        return best

    def attend_group(g):
        loads[g].wait()
        attend(range(g * GROUP, (g + 1) * GROUP))

    def stage(k):
        for slot, flag in ((k, me >= k), (replicas - k, me + k <= last)):
            @pl.when(flag)
            def _():
                send_idx[slot - 1].wait_recv()
                hot[0] = jnp.maximum(hot[0], homed(slot, range(STAY)))
        out_down[k - 1] = down_v[jnp.maximum(hot[0], 0)]
        start_if(me + k < last - 1, down_to(k, k))
        start_if(me - k > 1, down_to(replicas - k, k))
        if k > 1:
            start_if(me + k == last, down_to(k - 1, k))
            start_if(me == k, down_to(replicas - k + 1, k))

    for g in range(EARLY):
        attend_group(g)
    pl.semaphore_wait(barrier, replicas - 1 + tensors - 1 + jnp.where(proxy, tensors - 1, 0))

    for copy in send_idx:
        copy.start()
    for copy in send_rows:
        copy.start()
    hot[0] = homed(0, range(STAY))
    for g in range(EARLY, groups):
        attend_group(g)
    stay = jnp.where(stay_row < live[0], gather_rows(0, STAY), 0.0).astype(BF16)
    attention[0:STAY, :] = stay
    stay_out[...] = stay
    start_if(edge, send_stay)
    load_d.wait()
    load_u.wait()
    for k in range(1, replicas):
        stage(k)
    chosen = jnp.maximum(hot[0], 0)
    hot_down[0] = down_v[chosen]
    hot_up[0] = up_v[chosen]

    asked = jnp.full((replicas, 1), -1, jnp.int32)
    for d in range(replicas):
        asked = jnp.where(replica_row == d, homed(d, range(STAY, slots)), asked)
    for copy in send_rows:
        copy.wait_recv()
    rows = jnp.concatenate([row_in[d] for d in range(replicas)], axis=0).astype(BF16)
    partial = dot_nt(rows, down_v[...].reshape(count * rank, cols))
    owner = lax.broadcasted_iota(jnp.int32, partial.shape, 1) // rank
    rank_m[0] = jnp.where(owner == asked, partial, 0.0)
    for copy in send_tm:
        copy.start()

    for d in range(1, replicas):
        start_if(at_end(d), send_hu[d - 1])

    for copy in send_tm:
        copy.wait_recv()
    total = rank_m[0]
    for d in range(1, tensors):
        total = total + rank_m[d]
    made = widen(total, up_v[...].reshape(count * rank, cols)).astype(BF16).astype(F32)
    row_back[0] = made[0:1, :]
    for d in range(1, replicas):
        row_send[d] = made[d:d + 1, :]
    for copy in send_back:
        copy.start()
    for d in range(1, replicas):
        start_if(jnp.logical_not(at_end(d)), send_hu[d - 1])

    def by_home(buffer):
        return jnp.concatenate([buffer[lax.rem(me - h + replicas, replicas)] for h in range(replicas)], axis=0)

    def ranks(rows, home):
        partial = dot_nt(rows, by_home(hot_down))
        owner = lax.broadcasted_iota(jnp.int32, partial.shape, 1) // rank
        return jnp.where(owner == home, partial, 0.0)

    @pl.when(inner)
    def _():
        for d in range(1, replicas):
            down_to(d, 1).wait_recv()

    @pl.when(proxy)
    def _():
        send_stay.wait_recv()
        slot = jnp.where(me == 1, 1, last)
        home = jnp.zeros((STAY, 1), jnp.int32)
        for i in range(STAY):
            home = jnp.where(stay_row == i, index[slot, i] // count, home)
        rank_e[...] = ranks(stay_in[...], home)
        for copy in send_te:
            copy.start()

    @pl.when(inner)
    def _():
        rank_s[0] = ranks(stay_out[...], stay_home)
        for copy in send_ts:
            copy.start()

    for copy in send_back:
        copy.wait_recv()
    back = jnp.concatenate([row_back[d] for d in range(replicas)], axis=0)
    adapted[STAY:slots, :] = jnp.concatenate(
        [
            jnp.sum(jnp.where(replica_row == move_rel[j], back, 0.0), axis=0, keepdims=True)
            for j in range(moving)
        ],
        axis=0,
    ).astype(BF16)

    for copy in send_ts:
        copy.wait_recv()

    @pl.when(edge)
    def _():
        send_te[0].wait_recv()

    total = rank_s[0]
    for d in range(1, tensors):
        total = total + rank_s[d]
    for copy in send_hu:
        copy.wait_recv()
    adapted[0:STAY, :] = widen(total, by_home(hot_up)).astype(BF16)

    for copy in send_idx + send_rows + send_back + send_tm + send_hu:
        copy.wait_send()
    sent_if(edge, send_stay)
    for copy in send_ts:
        sent_if(inner, copy)
    for copy in send_te:
        sent_if(proxy, copy)
    for d in range(1, replicas):
        sent_if(jnp.logical_not(at_end(d)), down_to(d, 1))


def hand_over(attention, adapted, attention_out, adapted_out, sem):
    first = pltpu.make_async_copy(attention, attention_out, sem.at[0])
    second = pltpu.make_async_copy(adapted, adapted_out, sem.at[1])
    first.start()
    second.start()
    first.wait()
    second.wait()


def on_device(replicas, tensors, queries, past_cache, lengths, live_counts, adapter_index, adapter_down, adapter_up):
    slots, cols = queries.shape
    count, rank = adapter_down.shape[0], adapter_down.shape[1]
    heads = cols // HEAD_DIM
    out = jax.ShapeDtypeStruct((slots, cols), BF16)
    held = pltpu.VMEM((slots, cols), BF16)
    anywhere = pl.BlockSpec(memory_space=pl.ANY)
    vmem = pl.BlockSpec(memory_space=pltpu.VMEM)
    dma = pltpu.SemaphoreType.DMA
    rep = dma((max(replicas - 1, 1),))
    ten = dma((max(tensors - 1, 1),))
    all_ten = dma((tensors,))
    scratch = [
        pltpu.SMEM((slots,), jnp.int32),
        pltpu.SMEM((1,), jnp.int32),
        pltpu.SMEM((replicas, slots), jnp.int32),
        pltpu.SMEM((1,), jnp.int32),
        pltpu.VMEM((slots, cols), BF16),
        pltpu.VMEM(past_cache.shape, BF16),
        pltpu.VMEM(adapter_down.shape, BF16),
        pltpu.VMEM(adapter_up.shape, BF16),
        pltpu.VMEM((slots * heads, HEAD_DIM), F32),
        pltpu.VMEM((slots * heads, HEAD_DIM), F32),
        pltpu.VMEM((replicas, 1, cols), F32),
        pltpu.VMEM((replicas, 1, cols), F32),
        pltpu.VMEM((replicas, 1, cols), F32),
        pltpu.VMEM((replicas, 1, cols), F32),
        pltpu.VMEM((replicas - 1, rank, cols), BF16),
        pltpu.VMEM((replicas, rank, cols), BF16),
        pltpu.VMEM((replicas, rank, cols), BF16),
        pltpu.VMEM((STAY, cols), BF16),
        pltpu.VMEM((STAY, cols), BF16),
        pltpu.VMEM((tensors, replicas, count * rank), F32),
        pltpu.VMEM((tensors, STAY, replicas * rank), F32),
        pltpu.VMEM((STAY, replicas * rank), F32),
        dma((7,)),
        dma((STAY // GROUP,)),
        rep, rep, rep, rep, rep, rep, rep, rep, rep, rep, ten, ten, all_ten, all_ten, all_ten, dma(()), dma(()),
    ]
    results = pl.pallas_call(
        functools.partial(kernel, replicas, tensors),
        out_shape=(held, held),
        in_specs=[anywhere] * 7,
        out_specs=(vmem, vmem),
        scratch_shapes=scratch,
        compiler_params=pltpu.CompilerParams(collective_id=0, has_side_effects=True, vmem_limit_bytes=LIMIT),
    )(lengths, live_counts, adapter_index, queries, past_cache, adapter_down, adapter_up)
    return pl.pallas_call(
        hand_over,
        out_shape=(out, out),
        in_specs=[vmem, vmem],
        out_specs=(anywhere, anywhere),
        scratch_shapes=[dma((2,))],
        compiler_params=pltpu.CompilerParams(vmem_limit_bytes=4 * 1024 * 1024),
    )(*results)


def solution(mesh):
    in_specs = (
        P(("groups", "replica"), "tensor"),
        P(None, ("groups", "replica"), None, "tensor"),
        P(("groups", "replica")),
        P(("groups", "replica")),
        P(("groups", "replica")),
        P("replica", None, "tensor"),
        P("replica", None, "tensor"),
    )
    out_specs = (P(("groups", "replica"), "tensor"), P(("groups", "replica"), "tensor"))
    body = functools.partial(on_device, mesh.shape["replica"], mesh.shape["tensor"])
    return jax.shard_map(body, mesh=mesh, in_specs=in_specs, out_specs=out_specs, check_vma=False)
```

time: 24 us -> 21.3 us (0.89)
  Pallas kernels: 22.5 us -> 19.9 us
    pallas_call x1, Pallas kernels: 21.9 us -> 19.2 us  [on_device(): pl.pallas_call(functools.partial(kernel, replicas, tensors), out_shape=(h...]
where the time goes in v1:
time: 21.3 us; the launch traced here: 21.2 us
  Pallas kernels  19.9 us (93%)
  between operations  1.29 us (6%)
    pallas_call x1, Pallas kernels, on_device(): pl.pallas_call(functools.partial(kernel, replicas, tensors), out_shape=(h...  19.2 us
    pallas_call x1, Pallas kernels, on_device(): pl.pallas_call(hand_over, out_shape=(out, out), in_specs=[vmem, vmem], ou...  0.69 us

profile of v1, /device:TPU:0, one launch (start us, length us, event | category | flops | bytes accessed | tf_op | source)
XLA Modules:
  0.0 21.2 jit_solution(7594163864112921822)
XLA Ops:
  1.3 19.2 %shard_map.86 = (bf16[18,2048]{1,0:T(8,128)(2,1)S(1)}, bf16[18,2048]{1,0:T(8,128)(2,1)S(1)}) custom-call(s32[18]{0:T(128)} %lengths_in.1, s32[1]{0:T(128)S(6)} %copy.9.live_in, s32[18]{0:T(128)} %index_in.1, bf16[18,2048]{1,0:T(8,128)(2,1)} %queries.1, bf16[2,18,128,256]{3,2,1,0:T(8,128)(2,1)} %cache.1, bf16[4,16,2048]{2,1,0:T(8,128)(2,1)} %down.1, ...), custom_call_target="tpu_custom_call" | custom-call | tf_op jit(solution)/shard_map/pallas_call | solution.py:421
  20.5 0.7 %shard_map.87 = (bf16[18,2048]{1,0:T(8,128)(2,1)}, bf16[18,2048]{1,0:T(8,128)(2,1)}) custom-call(bf16[18,2048]{1,0:T(8,128)(2,1)S(1)} %get-tuple-element.4.attention, bf16[18,2048]{1,0:T(8,128)(2,1)S(1)} %get-tuple-element.5.adapted), custom_call_target="tpu_custom_call" | custom-call | tf_op jit(solution)/shard_map/pallas_call | solution.py:429

commit v2 on v1

--- a/solution.py
+++ b/solution.py
@@ -37,10 +37,10 @@
     replicas, tensors,
     lengths_in, live_in, index_in, queries, cache, down, up,
     attention, adapted,
-    lengths, live, index, hot, q_in, kv, down_v, up_v, q_rows, o_rows,
-    row_out, row_in, row_send, row_back, out_down, hot_down, hot_up, stay_out, stay_in, rank_m, rank_s, rank_e,
+    lengths, live, index, hot, q_in, kv, maps_v, q_rows, o_rows,
+    row_out, row_in, row_send, row_back, out_up, hot_down, hot_up, stay_in, rank_m, rank_out, rank_s,
     local_sem, group_sem,
-    idx_s, idx_r, row_s, row_r, back_s, back_r, hd_s, hd_r, hu_s, hu_r, tm_s, tm_r, ts_s, ts_r, te_s, st_s, st_r,
+    idx_s, idx_r, row_s, row_r, back_s, back_r, hd_s, hd_r, hu_s, hu_r, tm_s, tm_r, st_s, st_r, rs_s, rs_r,
 ):
     me = lax.axis_index("replica")
     mine = lax.axis_index("tensor")
@@ -52,12 +52,13 @@
     size = heads // key_heads
     count, rank = down.shape[0], down.shape[1]
     groups = STAY // GROUP
+    down_v, up_v = maps_v.at[0], maps_v.at[1]
     last = replicas - 1
-    edge = (me == 0) | (me == last)
-    inner = jnp.logical_not(edge)
-    proxy = (me == 1) | (me == last - 1)
-    helper = jnp.where(me == 0, 1, last - 1)
-    served = jnp.where(me == 1, 0, last)
+    half = replicas // 2
+    lower = me < half
+    base = jnp.where(lower, 0, half)
+    head = jnp.where(lower, half - 1, half)
+    leads = me == head
 
     def peer(offset):
         return {"replica": lax.rem(me + offset, replicas)}
@@ -71,12 +72,11 @@
     for d in range(1, tensors):
         pl.semaphore_signal(barrier, inc=1, device_id=side(d), device_id_type=MESH)
 
-    @pl.when(edge)
-    def _():
-        for d in range(1, tensors):
-            pl.semaphore_signal(
-                barrier, inc=1, device_id={"replica": helper, **side(d)}, device_id_type=MESH
-            )
+    for h in (half - 1, half):
+        @pl.when(me != h)
+        def _():
+            for d in range(1, tensors):
+                pl.semaphore_signal(barrier, inc=1, device_id={"replica": h, **side(d)}, device_id_type=MESH)
 
     load_i = pltpu.make_async_copy(index_in, index.at[0], local_sem.at[0])
     load_n = pltpu.make_async_copy(lengths_in, lengths, local_sem.at[1])
@@ -105,11 +105,11 @@
     for copy in loads[2:]:
         copy.start()
 
-    def to_peers(source, target, send, recv):
+    def to_peers(source, target, send, recv, own=False):
         return [
             pltpu.make_async_remote_copy(
-                src_ref=source(d), dst_ref=target.at[d], send_sem=send.at[d - 1],
-                recv_sem=recv.at[d - 1], device_id=peer(d), device_id_type=MESH,
+                src_ref=source(d), dst_ref=target.at[d], send_sem=send.at[0],
+                recv_sem=recv.at[d - 1 if own else 0], device_id=peer(d), device_id_type=MESH,
             )
             for d in range(1, replicas)
         ]
@@ -117,51 +117,49 @@
     def to_sides(buffer, send, recv):
         return [
             pltpu.make_async_remote_copy(
-                src_ref=buffer.at[0], dst_ref=buffer.at[d], send_sem=send.at[d - 1],
-                recv_sem=recv.at[d - 1], device_id=side(d), device_id_type=MESH,
+                src_ref=buffer.at[0], dst_ref=buffer.at[d], send_sem=send.at[0],
+                recv_sem=recv.at[0], device_id=side(d), device_id_type=MESH,
             )
             for d in range(1, tensors)
         ]
 
-    send_idx = to_peers(lambda d: index.at[0], index, idx_s, idx_r)
+    def drain(ref, sem):
+        pltpu.make_async_copy(ref, ref, sem.at[0]).wait()
+
+    send_idx = to_peers(lambda d: index.at[0], index, idx_s, idx_r, own=True)
     send_rows = to_peers(lambda d: row_out.at[d], row_in, row_s, row_r)
     send_back = [
         pltpu.make_async_remote_copy(
-            src_ref=row_send.at[d], dst_ref=row_back.at[d], send_sem=back_s.at[d - 1],
-            recv_sem=back_r.at[d - 1], device_id=peer(replicas - d), device_id_type=MESH,
+            src_ref=row_send.at[d], dst_ref=row_back.at[d], send_sem=back_s.at[0],
+            recv_sem=back_r.at[0], device_id=peer(replicas - d), device_id_type=MESH,
         )
         for d in range(1, replicas)
     ]
     send_tm = to_sides(rank_m, tm_s, tm_r)
-    send_ts = [
-        pltpu.make_async_remote_copy(
-            src_ref=rank_s.at[0], dst_ref=rank_s.at[d], send_sem=ts_s.at[d],
-            recv_sem=ts_r.at[d], device_id=side(d), device_id_type=MESH,
-        )
-        for d in range(1, tensors)
-    ]
-    send_te = [
-        pltpu.make_async_remote_copy(
-            src_ref=rank_e, dst_ref=rank_s.at[d], send_sem=te_s.at[d],
-            recv_sem=ts_r.at[d], device_id={"replica": served, **side(d)}, device_id_type=MESH,
-        )
-        for d in range(tensors)
-    ]
-    send_stay = pltpu.make_async_remote_copy(
-        src_ref=stay_out, dst_ref=stay_in, send_sem=st_s, recv_sem=st_r,
-        device_id={"replica": helper}, device_id_type=MESH,
+    def stay_to(h):
+        return pltpu.make_async_remote_copy(
+            src_ref=stay_in.at[0], dst_ref=stay_in.at[lax.rem(h - me + replicas, replicas)], send_sem=st_s.at[0],
+            recv_sem=st_r.at[0], device_id={"replica": h}, device_id_type=MESH,
+        )
+
+    send_down = pltpu.make_async_remote_copy(
+        src_ref=hot_down.at[me - base], dst_ref=hot_down.at[me - base], send_sem=hd_s.at[0],
+        recv_sem=hd_r.at[0], device_id={"replica": head}, device_id_type=MESH,
     )
-    send_hu = to_peers(lambda d: hot_up.at[0], hot_up, hu_s, hu_r)
-
-    def down_to(d, k):
+
+    def ranks_to(d, t):
+        side_slot = jnp.where(lower, 0, tensors) + t
         return pltpu.make_async_remote_copy(
-            src_ref=out_down.at[k - 1], dst_ref=hot_down.at[d], send_sem=hd_s.at[d - 1],
-            recv_sem=hd_r.at[d - 1], device_id=peer(d), device_id_type=MESH,
-        )
-
-    def at_end(d):
-        target = lax.rem(me + d, replicas)
-        return (target == 0) | (target == last)
+            src_ref=rank_out.at[d], dst_ref=rank_s.at[side_slot], send_sem=rs_s.at[t],
+            recv_sem=rs_r.at[0], device_id={"replica": lax.rem(me - d + replicas, replicas), **side(t)},
+            device_id_type=MESH,
+        )
+
+    def up_to(d, source):
+        return pltpu.make_async_remote_copy(
+            src_ref=source, dst_ref=hot_up.at[d], send_sem=hu_s.at[0],
+            recv_sem=hu_r.at[0], device_id=peer(d), device_id_type=MESH,
+        )
 
     def start_if(flag, copy):
         @pl.when(flag)
@@ -245,16 +243,14 @@
             def _():
                 send_idx[slot - 1].wait_recv()
                 hot[0] = jnp.maximum(hot[0], homed(slot, range(STAY)))
-        out_down[k - 1] = down_v[jnp.maximum(hot[0], 0)]
-        start_if(me + k < last - 1, down_to(k, k))
-        start_if(me - k > 1, down_to(replicas - k, k))
-        if k > 1:
-            start_if(me + k == last, down_to(k - 1, k))
-            start_if(me == k, down_to(replicas - k + 1, k))
+        out_up[k - 1] = up_v[jnp.maximum(hot[0], 0)]
+        other = jnp.where(lower, half, half - 1)
+        start_if(leads & (me + k <= last) & (me + k != other), up_to(k, out_up.at[k - 1]))
+        start_if(leads & (me >= k) & (me - k != other), up_to(replicas - k, out_up.at[k - 1]))
 
     for g in range(EARLY):
         attend_group(g)
-    pl.semaphore_wait(barrier, replicas - 1 + tensors - 1 + jnp.where(proxy, tensors - 1, 0))
+    pl.semaphore_wait(barrier, jnp.where(leads, replicas * tensors - 1, replicas + tensors - 2))
 
     for copy in send_idx:
         copy.start()
@@ -265,21 +261,29 @@
         attend_group(g)
     stay = jnp.where(stay_row < live[0], gather_rows(0, STAY), 0.0).astype(BF16)
     attention[0:STAY, :] = stay
-    stay_out[...] = stay
-    start_if(edge, send_stay)
+    stay_in[0] = stay
+    for h in (half - 1, half):
+        start_if(me != h, stay_to(h))
     load_d.wait()
     load_u.wait()
     for k in range(1, replicas):
         stage(k)
     chosen = jnp.maximum(hot[0], 0)
-    hot_down[0] = down_v[chosen]
+    hot_down[me - base] = down_v[chosen]
     hot_up[0] = up_v[chosen]
+    start_if(jnp.logical_not(leads), send_down)
+    for step in range(1, replicas):
+        far = replicas - step
+        start_if(jnp.logical_not(leads) & lower & (me + far <= last), up_to(far, hot_up.at[0]))
+        start_if(jnp.logical_not(leads) & jnp.logical_not(lower) & (me >= far), up_to(replicas - far, hot_up.at[0]))
+    for step in range(1, half):
+        start_if(jnp.logical_not(leads) & lower & (me >= step), up_to(replicas - step, hot_up.at[0]))
+        start_if(jnp.logical_not(leads) & jnp.logical_not(lower) & (me + step <= last), up_to(step, hot_up.at[0]))
 
     asked = jnp.full((replicas, 1), -1, jnp.int32)
     for d in range(replicas):
         asked = jnp.where(replica_row == d, homed(d, range(STAY, slots)), asked)
-    for copy in send_rows:
-        copy.wait_recv()
+    drain(row_in.at[pl.ds(1, last)], row_r)
     rows = jnp.concatenate([row_in[d] for d in range(replicas)], axis=0).astype(BF16)
     partial = dot_nt(rows, down_v[...].reshape(count * rank, cols))
     owner = lax.broadcasted_iota(jnp.int32, partial.shape, 1) // rank
@@ -287,11 +291,14 @@
     for copy in send_tm:
         copy.start()
 
-    for d in range(1, replicas):
-        start_if(at_end(d), send_hu[d - 1])
-
-    for copy in send_tm:
-        copy.wait_recv()
+    homes = []
+    for d in range(replicas):
+        home = jnp.zeros((STAY, 1), jnp.int32)
+        for i in range(STAY):
+            home = jnp.where(stay_row == i, index[d, i] // count, home)
+        homes.append(home)
+    homes = jnp.concatenate(homes, axis=0) - base
+    drain(rank_m.at[pl.ds(1, tensors - 1)], tm_r)
     total = rank_m[0]
     for d in range(1, tensors):
         total = total + rank_m[d]
@@ -301,41 +308,29 @@
         row_send[d] = made[d:d + 1, :]
     for copy in send_back:
         copy.start()
-    for d in range(1, replicas):
-        start_if(jnp.logical_not(at_end(d)), send_hu[d - 1])
-
-    def by_home(buffer):
-        return jnp.concatenate([buffer[lax.rem(me - h + replicas, replicas)] for h in range(replicas)], axis=0)
-
-    def ranks(rows, home):
-        partial = dot_nt(rows, by_home(hot_down))
+    part = half * rank
+    lines = STAY // 2
+
+    @pl.when(leads)
+    def _():
+        drain(stay_in.at[pl.ds(1, last)], st_r)
+        if half > 1:
+            drain(hot_down.at[pl.ds(1, half - 1)], hd_r)
+        partial = dot_nt(stay_in[...].reshape(replicas * STAY, cols), hot_down[...].reshape(part, cols))
         owner = lax.broadcasted_iota(jnp.int32, partial.shape, 1) // rank
-        return jnp.where(owner == home, partial, 0.0)
-
-    @pl.when(inner)
-    def _():
-        for d in range(1, replicas):
-            down_to(d, 1).wait_recv()
-
-    @pl.when(proxy)
-    def _():
-        send_stay.wait_recv()
-        slot = jnp.where(me == 1, 1, last)
-        home = jnp.zeros((STAY, 1), jnp.int32)
-        for i in range(STAY):
-            home = jnp.where(stay_row == i, index[slot, i] // count, home)
-        rank_e[...] = ranks(stay_in[...], home)
-        for copy in send_te:
-            copy.start()
-
-    @pl.when(inner)
-    def _():
-        rank_s[0] = ranks(stay_out[...], stay_home)
-        for copy in send_ts:
-            copy.start()
-
-    for copy in send_back:
-        copy.wait_recv()
+        partial = jnp.where(owner == homes, partial, 0.0)
+        for d in range(replicas):
+            block = partial[d * STAY:(d + 1) * STAY]
+            rank_out[d] = jnp.concatenate([block[:lines], block[lines:]], axis=1)
+        rank_s[jnp.where(lower, 0, tensors)] = rank_out[0]
+        for d in range(replicas):
+            for t in range(tensors):
+                if d or t:
+                    ranks_to(d, t).start()
+        start_if(lower, up_to(1, hot_up.at[0]))
+        start_if(jnp.logical_not(lower), up_to(last, hot_up.at[0]))
+
+    drain(row_back.at[pl.ds(1, last)], back_r)
     back = jnp.concatenate([row_back[d] for d in range(replicas)], axis=0)
     adapted[STAY:slots, :] = jnp.concatenate(
         [
@@ -345,29 +340,42 @@
         axis=0,
     ).astype(BF16)
 
-    for copy in send_ts:
-        copy.wait_recv()
-
-    @pl.when(edge)
+    @pl.when(leads)
     def _():
-        send_te[0].wait_recv()
-
-    total = rank_s[0]
-    for d in range(1, tensors):
-        total = total + rank_s[d]
-    for copy in send_hu:
-        copy.wait_recv()
-    adapted[0:STAY, :] = widen(total, by_home(hot_up)).astype(BF16)
-
-    for copy in send_idx + send_rows + send_back + send_tm + send_hu:
-        copy.wait_send()
-    sent_if(edge, send_stay)
-    for copy in send_ts:
-        sent_if(inner, copy)
-    for copy in send_te:
-        sent_if(proxy, copy)
-    for d in range(1, replicas):
-        sent_if(jnp.logical_not(at_end(d)), down_to(d, 1))
+        drain(rank_s.at[pl.ds(1, 2 * tensors - 1)], rs_r)
+
+    @pl.when(jnp.logical_not(leads))
+    def _():
+        drain(rank_s, rs_r)
+
+    totals = []
+    for side_slot in (0, tensors):
+        total = rank_s[side_slot]
+        for d in range(1, tensors):
+            total = total + rank_s[side_slot + d]
+        totals.append(jnp.concatenate([total[:, :part], total[:, part:]], axis=0))
+    total = jnp.concatenate(totals, axis=1)
+    drain(hot_up.at[pl.ds(1, last)], hu_r)
+    ups = jnp.concatenate([hot_up[lax.rem(me - h + replicas, replicas)] for h in range(replicas)], axis=0)
+    adapted[0:STAY, :] = widen(total, ups).astype(BF16)
+
+    drain(index.at[pl.ds(1, last)], idx_s)
+    drain(row_out.at[pl.ds(1, last)], row_s)
+    drain(row_send.at[pl.ds(1, last)], back_s)
+    drain(rank_m.at[pl.ds(1, tensors - 1)], tm_s)
+    drain(hot_up.at[pl.ds(1, last)], hu_s)
+
+    @pl.when(leads)
+    def _():
+        drain(stay_in.at[0], st_s)
+        drain(rank_out.at[pl.ds(1, last)], rs_s.at[pl.ds(0, 1)])
+        for t in range(1, tensors):
+            drain(rank_out, rs_s.at[pl.ds(t, 1)])
+
+    @pl.when(jnp.logical_not(leads))
+    def _():
+        drain(stay_in.at[pl.ds(0, 2)], st_s)
+        drain(hot_down.at[0], hd_s)
 
 
 def hand_over(attention, adapted, attention_out, adapted_out, sem):
@@ -388,9 +396,10 @@
     anywhere = pl.BlockSpec(memory_space=pl.ANY)
     vmem = pl.BlockSpec(memory_space=pltpu.VMEM)
     dma = pltpu.SemaphoreType.DMA
-    rep = dma((max(replicas - 1, 1),))
-    ten = dma((max(tensors - 1, 1),))
-    all_ten = dma((tensors,))
+    rep = dma((replicas - 1,))
+    one = dma((1,))
+    ten = dma((tensors,))
+    half = replicas // 2
     scratch = [
         pltpu.SMEM((slots,), jnp.int32),
         pltpu.SMEM((1,), jnp.int32),
@@ -398,8 +407,7 @@
         pltpu.SMEM((1,), jnp.int32),
         pltpu.VMEM((slots, cols), BF16),
         pltpu.VMEM(past_cache.shape, BF16),
-        pltpu.VMEM(adapter_down.shape, BF16),
-        pltpu.VMEM(adapter_up.shape, BF16),
+        pltpu.VMEM((2, *adapter_down.shape), BF16),
         pltpu.VMEM((slots * heads, HEAD_DIM), F32),
         pltpu.VMEM((slots * heads, HEAD_DIM), F32),
         pltpu.VMEM((replicas, 1, cols), F32),
@@ -407,16 +415,15 @@
         pltpu.VMEM((replicas, 1, cols), F32),
         pltpu.VMEM((replicas, 1, cols), F32),
         pltpu.VMEM((replicas - 1, rank, cols), BF16),
+        pltpu.VMEM((half, rank, cols), BF16),
         pltpu.VMEM((replicas, rank, cols), BF16),
-        pltpu.VMEM((replicas, rank, cols), BF16),
-        pltpu.VMEM((STAY, cols), BF16),
-        pltpu.VMEM((STAY, cols), BF16),
+        pltpu.VMEM((replicas, STAY, cols), BF16),
         pltpu.VMEM((tensors, replicas, count * rank), F32),
-        pltpu.VMEM((tensors, STAY, replicas * rank), F32),
-        pltpu.VMEM((STAY, replicas * rank), F32),
+        pltpu.VMEM((replicas, STAY // 2, replicas * rank), F32),
+        pltpu.VMEM((2 * tensors, STAY // 2, replicas * rank), F32),
         dma((7,)),
         dma((STAY // GROUP,)),
-        rep, rep, rep, rep, rep, rep, rep, rep, rep, rep, ten, ten, all_ten, all_ten, all_ten, dma(()), dma(()),
+        one, rep, one, one, one, one, one, one, one, one, one, one, one, one, ten, one,
     ]
     results = pl.pallas_call(
         functools.partial(kernel, replicas, tensors),

time: 21.3 us -> 20.9 us (0.981)
  Pallas kernels: 19.9 us -> 19.5 us
    pallas_call x1, Pallas kernels: 19.2 us -> 18.8 us  [on_device(): pl.pallas_call(functools.partial(kernel, replicas, tensors), out_shape=(h...]
where the time goes in v2:
time: 20.9 us; the launch traced here: 20.8 us
  Pallas kernels  19.5 us (93%)
  between operations  1.29 us (6%)
    pallas_call x1, Pallas kernels, on_device(): pl.pallas_call(functools.partial(kernel, replicas, tensors), out_shape=(h...  18.8 us
    pallas_call x1, Pallas kernels, on_device(): pl.pallas_call(hand_over, out_shape=(out, out), in_specs=[vmem, vmem], ou...  0.69 us

profile of v2, /device:TPU:0, one launch (start us, length us, event | category | flops | bytes accessed | tf_op | source)
XLA Modules:
  0.0 20.8 jit_solution(15624021062828056864)
XLA Ops:
  1.3 18.8 %shard_map.86 = (bf16[18,2048]{1,0:T(8,128)(2,1)S(1)}, bf16[18,2048]{1,0:T(8,128)(2,1)S(1)}) custom-call(s32[18]{0:T(128)} %lengths_in.1, s32[1]{0:T(128)S(6)} %copy.9.live_in, s32[18]{0:T(128)} %index_in.1, bf16[18,2048]{1,0:T(8,128)(2,1)} %queries.1, bf16[2,18,128,256]{3,2,1,0:T(8,128)(2,1)} %cache.1, bf16[4,16,2048]{2,1,0:T(8,128)(2,1)} %down.1, ...), custom_call_target="tpu_custom_call" | custom-call | tf_op jit(solution)/shard_map/pallas_call | solution.py:428
  20.1 0.7 %shard_map.87 = (bf16[18,2048]{1,0:T(8,128)(2,1)}, bf16[18,2048]{1,0:T(8,128)(2,1)}) custom-call(bf16[18,2048]{1,0:T(8,128)(2,1)S(1)} %get-tuple-element.4.attention, bf16[18,2048]{1,0:T(8,128)(2,1)S(1)} %get-tuple-element.5.adapted), custom_call_target="tpu_custom_call" | custom-call | tf_op jit(solution)/shard_map/pallas_call | solution.py:436

commit v3 on v2

--- a/solution.py
+++ b/solution.py
@@ -12,7 +12,7 @@
 STAY = 16
 SCALING = 2.0
 GROUP = 8
-EARLY = 1
+EARLY = 0
 LIMIT = 67043328 - 240 * 1024
 MESH = pl.DeviceIdType.MESH
 F32 = jnp.float32
@@ -72,11 +72,14 @@
     for d in range(1, tensors):
         pl.semaphore_signal(barrier, inc=1, device_id=side(d), device_id_type=MESH)
 
-    for h in (half - 1, half):
-        @pl.when(me != h)
-        def _():
-            for d in range(1, tensors):
-                pl.semaphore_signal(barrier, inc=1, device_id={"replica": h, **side(d)}, device_id_type=MESH)
+    odd = lax.rem(mine, 2) == 1
+
+    @pl.when(jnp.logical_not(odd))
+    def _():
+        for d in range(1, replicas):
+            pl.semaphore_signal(
+                barrier, inc=1, device_id={**peer(d), "tensor": mine + 1}, device_id_type=MESH
+            )
 
     load_i = pltpu.make_async_copy(index_in, index.at[0], local_sem.at[0])
     load_n = pltpu.make_async_copy(lengths_in, lengths, local_sem.at[1])
@@ -105,11 +108,11 @@
     for copy in loads[2:]:
         copy.start()
 
-    def to_peers(source, target, send, recv, own=False):
+    def to_peers(source, target, send, recv):
         return [
             pltpu.make_async_remote_copy(
                 src_ref=source(d), dst_ref=target.at[d], send_sem=send.at[0],
-                recv_sem=recv.at[d - 1 if own else 0], device_id=peer(d), device_id_type=MESH,
+                recv_sem=recv.at[0], device_id=peer(d), device_id_type=MESH,
             )
             for d in range(1, replicas)
         ]
@@ -126,7 +129,12 @@
     def drain(ref, sem):
         pltpu.make_async_copy(ref, ref, sem.at[0]).wait()
 
-    send_idx = to_peers(lambda d: index.at[0], index, idx_s, idx_r, own=True)
+    def index_to(d, back):
+        return pltpu.make_async_remote_copy(
+            src_ref=index.at[0], dst_ref=index.at[d], send_sem=idx_s.at[0], recv_sem=idx_r.at[d - 1],
+            device_id={**peer(d), "tensor": mine - back}, device_id_type=MESH,
+        )
+
     send_rows = to_peers(lambda d: row_out.at[d], row_in, row_s, row_r)
     send_back = [
         pltpu.make_async_remote_copy(
@@ -241,7 +249,7 @@
         for slot, flag in ((k, me >= k), (replicas - k, me + k <= last)):
             @pl.when(flag)
             def _():
-                send_idx[slot - 1].wait_recv()
+                index_to(slot, 0).wait_recv()
                 hot[0] = jnp.maximum(hot[0], homed(slot, range(STAY)))
         out_up[k - 1] = up_v[jnp.maximum(hot[0], 0)]
         other = jnp.where(lower, half, half - 1)
@@ -250,10 +258,11 @@
 
     for g in range(EARLY):
         attend_group(g)
-    pl.semaphore_wait(barrier, jnp.where(leads, replicas * tensors - 1, replicas + tensors - 2))
-
-    for copy in send_idx:
-        copy.start()
+    pl.semaphore_wait(barrier, jnp.where(odd, 2 * replicas + tensors - 3, replicas + tensors - 2))
+
+    for d in range(1, replicas):
+        start_if(odd, index_to(d, 1))
+        start_if(odd, index_to(d, 0))
     for copy in send_rows:
         copy.start()
     hot[0] = homed(0, range(STAY))
@@ -272,13 +281,15 @@
     hot_down[me - base] = down_v[chosen]
     hot_up[0] = up_v[chosen]
     start_if(jnp.logical_not(leads), send_down)
+    near = lax.rem(head - me + replicas, replicas)
     for step in range(1, replicas):
         far = replicas - step
-        start_if(jnp.logical_not(leads) & lower & (me + far <= last), up_to(far, hot_up.at[0]))
-        start_if(jnp.logical_not(leads) & jnp.logical_not(lower) & (me >= far), up_to(replicas - far, hot_up.at[0]))
+        start_if(jnp.logical_not(leads) & lower & (me + far <= last) & (far != near), up_to(far, hot_up.at[0]))
+        back_by = replicas - far
+        start_if(jnp.logical_not(leads | lower) & (me >= far) & (back_by != near), up_to(back_by, hot_up.at[0]))
     for step in range(1, half):
         start_if(jnp.logical_not(leads) & lower & (me >= step), up_to(replicas - step, hot_up.at[0]))
-        start_if(jnp.logical_not(leads) & jnp.logical_not(lower) & (me + step <= last), up_to(step, hot_up.at[0]))
+        start_if(jnp.logical_not(leads | lower) & (me + step <= last), up_to(step, hot_up.at[0]))
 
     asked = jnp.full((replicas, 1), -1, jnp.int32)
     for d in range(replicas):
@@ -308,6 +319,9 @@
         row_send[d] = made[d:d + 1, :]
     for copy in send_back:
         copy.start()
+    for d in range(1, replicas):
+        start_if(jnp.logical_not(leads) & (near == d), up_to(d, hot_up.at[0]))
+
     part = half * rank
     lines = STAY // 2
 
@@ -359,7 +373,11 @@
     ups = jnp.concatenate([hot_up[lax.rem(me - h + replicas, replicas)] for h in range(replicas)], axis=0)
     adapted[0:STAY, :] = widen(total, ups).astype(BF16)
 
-    drain(index.at[pl.ds(1, last)], idx_s)
+    @pl.when(odd)
+    def _():
+        drain(index.at[pl.ds(1, last)], idx_s)
+        drain(index.at[pl.ds(1, last)], idx_s)
+
     drain(row_out.at[pl.ds(1, last)], row_s)
     drain(row_send.at[pl.ds(1, last)], back_s)
     drain(rank_m.at[pl.ds(1, tensors - 1)], tm_s)

time: 20.9 us -> 20.7 us (level)
  Pallas kernels: 19.5 us -> 19.2 us
    pallas_call x1, Pallas kernels: 18.8 us -> 18.5 us  [on_device(): pl.pallas_call(functools.partial(kernel, replicas, tensors), out_shape=(h...]
where the time goes in v3:
time: 20.7 us; the launch traced here: 20.5 us
  Pallas kernels  19.2 us (93%)
  between operations  1.29 us (6%)
    pallas_call x1, Pallas kernels, on_device(): pl.pallas_call(functools.partial(kernel, replicas, tensors), out_shape=(h...  18.5 us
    pallas_call x1, Pallas kernels, on_device(): pl.pallas_call(hand_over, out_shape=(out, out), in_specs=[vmem, vmem], ou...  0.69 us

profile of v3, /device:TPU:0, one launch (start us, length us, event | category | flops | bytes accessed | tf_op | source)
XLA Modules:
  0.0 20.5 jit_solution(3876111708143375064)
XLA Ops:
  1.3 18.5 %shard_map.86 = (bf16[18,2048]{1,0:T(8,128)(2,1)S(1)}, bf16[18,2048]{1,0:T(8,128)(2,1)S(1)}) custom-call(s32[18]{0:T(128)} %lengths_in.1, s32[1]{0:T(128)S(6)} %copy.9.live_in, s32[18]{0:T(128)} %index_in.1, bf16[18,2048]{1,0:T(8,128)(2,1)} %queries.1, bf16[2,18,128,256]{3,2,1,0:T(8,128)(2,1)} %cache.1, bf16[4,16,2048]{2,1,0:T(8,128)(2,1)} %down.1, ...), custom_call_target="tpu_custom_call" | custom-call | tf_op jit(solution)/shard_map/pallas_call | solution.py:446
  19.8 0.7 %shard_map.87 = (bf16[18,2048]{1,0:T(8,128)(2,1)}, bf16[18,2048]{1,0:T(8,128)(2,1)}) custom-call(bf16[18,2048]{1,0:T(8,128)(2,1)S(1)} %get-tuple-element.4.attention, bf16[18,2048]{1,0:T(8,128)(2,1)S(1)} %get-tuple-element.5.adapted), custom_call_target="tpu_custom_call" | custom-call | tf_op jit(solution)/shard_map/pallas_call | solution.py:454
